TPU v7x, 32 devices: a whole 2x2x4 slice. The times are simulated.
32 devices in a mesh: tm: 8 (over y, x, core), space: 4 (over z).
Axes of the slice: x: 2, y: 2, z: 4, core: 2. Of those that a mesh axis runs over, the one named last changes fastest.
Arguments:
- initial_state: float32 [192, 512], P('space'), may hold values from -6 to 6
- velocity: bfloat16 [192, 512], P('space'), may hold values from -0.5 to 0.5
- diffusion: bfloat16 [192, 512], P('space'), may hold values from 0.25 to 0.5
- forcing: bfloat16 [64, 192, 512], P('tm', 'space'), may hold values from -6 to 6
- implicit: float32 [512, 512], replicated, may hold values from 0 to 1
- coarse_implicit: float32 [512, 512], replicated, may hold values from 0 to 1
Outputs:
- solution: float32 [64, 192, 512], P('tm', 'space')
All inputs are finite; a program needn't handle non-finite values.
Results may differ from a plain program's by a relative error of at most 0.0003.
Values may be sent and summed in bfloat16 or wider, within the bound.
No kernel may reach another device: no remote copies, remote signals or barrier semaphores. Data moves between devices by JAX's collectives and lax.ppermute only.
A program may use at most 64 MiB of HBM per device.

v0:
```python
import jax
import jax.numpy as jnp
from jax import lax
from jax.sharding import PartitionSpec as P

CYCLES = 2
HIGHEST = lax.Precision.HIGHEST


def with_halo(cells, sides, width):
    for axis, dim in sides:
        count = lax.axis_size(axis)
        head = lax.slice_in_dim(cells, 0, width, axis=dim)
        tail = lax.slice_in_dim(cells, cells.shape[dim] - width, cells.shape[dim], axis=dim)
        cells = jnp.concatenate(
            [
                lax.ppermute(tail, axis, [(i, (i + 1) % count) for i in range(count)]),
                cells,
                lax.ppermute(head, axis, [((i + 1) % count, i) for i in range(count)]),
            ],
            axis=dim,
        )
    return cells


def from_behind(block, axis, distance):
    devices = range(lax.axis_size(axis))
    route = [(i - distance, i) for i in devices if i - distance in devices]
    return lax.ppermute(block, axis, route)


def stencil_weights(velocity, diffusion):
    moving = velocity.astype(jnp.float32)
    spread = diffusion.astype(jnp.float32)
    return (spread + 0.5 * moving, 1.0 - 2.0 * spread, spread - 0.5 * moving)


def apply_matrix(field, matrix):
    return jnp.dot(field, matrix, precision=HIGHEST, preferred_element_type=jnp.float32)


def per_device(initial_state, velocity, diffusion, forcing, implicit, coarse_implicit):
    slab_rows = initial_state.shape[0]
    block_steps = forcing.shape[0]
    first_block = lax.axis_index("tm") == 0
    stacked = jnp.concatenate([forcing, velocity[None], diffusion[None]], axis=0)
    sources = with_halo(stacked, (("space", 1),), block_steps)
    wide_weights = stencil_weights(sources[block_steps], sources[block_steps + 1])
    wide_forcing = sources[:block_steps]

    def relax_block(begin_state, step_count):
        values = []
        current = with_halo(begin_state, (("space", 0),), block_steps)
        width_all = current.shape[0]
        for offset in range(1, step_count + 1):
            upper_edge = width_all - offset
            summed = (
                wide_weights[1][offset:upper_edge] * current[1:-1]
                + wide_weights[2][offset:upper_edge] * current[2:]
                + wide_weights[0][offset:upper_edge] * current[:-2]
                + wide_forcing[offset - 1, offset:upper_edge].astype(jnp.float32)
            )
            current = apply_matrix(summed, implicit)
            values.append(current[block_steps - offset : block_steps - offset + slab_rows])
        return values

    def previous(end_values):
        arrived = from_behind(end_values, "tm", 1)
        return jnp.where(first_block, initial_state, arrived)

    end_values = jnp.zeros_like(initial_state)
    for repeat in range(CYCLES):
        if repeat == 0:
            begin_state = jnp.where(first_block, initial_state, jnp.zeros_like(initial_state))
        else:
            begin_state = previous(end_values)
        end_values = relax_block(begin_state, block_steps)[-1]
        residual = relax_block(previous(end_values), block_steps)[-1] - end_values
        gathered = lax.all_gather(
            residual[None].astype(jnp.bfloat16), "tm", axis=0, tiled=True
        ).astype(jnp.float32)

        def coarse_turn(source, carried):
            return apply_matrix(carried, coarse_implicit) + gathered[source]

        end_values = end_values + lax.fori_loop(
            1, lax.axis_index("tm") + 1, coarse_turn, gathered[0]
        )
    values = relax_block(previous(end_values), block_steps - 1)
    return jnp.stack(values + [end_values], axis=0)


def solution(mesh):
    in_specs = (
        P("space", None),
        P("space", None),
        P("space", None),
        P("tm", "space", None),
        P(),
        P(),
    )
    out_specs = P("tm", "space", None)
    return jax.shard_map(
        per_device, mesh=mesh, in_specs=in_specs, out_specs=out_specs, check_vma=False
    )
```

profile of v0, /device:TPU:6, one launch (start us, length us, event | category | flops | bytes accessed | tf_op | source)
XLA Modules:
  0.0 139.8 jit_solution(8762002623819105948)
XLA Ops:
  0.1 3.7 %collective-permute-start.3 = (f32[8,512]{1,0:T(8,128)S(1)}, f32[8,512]{1,0:T(8,128)S(1)}, u32[]{:S(2)}, u32[]{:S(2)}) collective-permute-start(f32[8,512]{1,0:T(8,128)S(1)} %get-tuple-element.102), channel_id=1, source_target_pairs={{1,0},{2,1},{3,2},{0,3},{5,4},{6,5},{7,6},{4,7},{9,8},{10,9},{11,1... | collective-permute-start | bytes 49160 | tf_op jit(solution)/shard_map/ppermute | solution.py:19
  4.7 3.9 %collective-permute-start.1 = (bf16[10,8,512]{2,1,0:T(8,128)(2,1)S(1)}, bf16[10,8,512]{2,1,0:T(8,128)(2,1)S(1)}, u32[]{:S(2)}, u32[]{:S(2)}) collective-permute-start(bf16[10,8,512]{2,1,0:T(8,128)(2,1)S(1)} %get-tuple-element.89), channel_id=1, source_target_pairs={{1,0},{2,1},{3,2},{0,3},{5,4},{6,5},{7,6},{4,7},{9,8},{10,9},{11,1... | collective-permute-start | bytes 245768 | tf_op jit(solution)/shard_map/ppermute | solution.py:19
  10.6 4.2 %collective-permute-done = bf16[10,8,512]{2,1,0:T(8,128)(2,1)S(1)} collective-permute-done((bf16[10,8,512]{2,1,0:T(8,128)(2,1)S(1)}, bf16[10,8,512]{2,1,0:T(8,128)(2,1)S(1)}, u32[]{:S(2)}, u32[]{:S(2)}) %collective-permute-start) | collective-permute-done | bytes 81952 | tf_op jit(solution)/shard_map/ppermute | solution.py:17
  22.2 1.9 %collective-permute-start.4 = (f32[48,512]{1,0:T(8,128)S(1)}, f32[48,512]{1,0:T(8,128)S(1)}, u32[]{:S(2)}, u32[]{:S(2)}) collective-permute-start(f32[48,512]{1,0:T(8,128)S(1)} %fusion.182), channel_id=1, source_target_pairs={{0,4},{4,8},{8,12},{12,16},{16,20},{20,24},{24,28},{1,5},{5,9},{9,... | collective-permute-start | bytes 294920 | tf_op jit(solution)/shard_map/ppermute | solution.py:29
  24.1 4.0 %collective-permute-done.4 = f32[48,512]{1,0:T(8,128)S(1)} collective-permute-done((f32[48,512]{1,0:T(8,128)S(1)}, f32[48,512]{1,0:T(8,128)S(1)}, u32[]{:S(2)}, u32[]{:S(2)}) %collective-permute-start.4) | collective-permute-done | bytes 98336 | tf_op jit(solution)/shard_map/ppermute | solution.py:29
  28.3 2.0 %collective-permute-start.5 = (f32[8,512]{1,0:T(8,128)S(1)}, f32[8,512]{1,0:T(8,128)S(1)}, u32[]{:S(2)}, u32[]{:S(2)}) collective-permute-start(f32[8,512]{1,0:T(8,128)S(1)} %get-tuple-element.99), channel_id=1, source_target_pairs={{0,1},{1,2},{2,3},{3,0},{4,5},{5,6},{6,7},{7,4},{8,9},{9,10},{10,1... | collective-permute-start | bytes 49160 | tf_op jit(solution)/shard_map/ppermute | solution.py:17
  30.2 1.7 %collective-permute-done.6 = f32[8,512]{1,0:T(8,128)S(1)} collective-permute-done((f32[8,512]{1,0:T(8,128)S(1)}, f32[8,512]{1,0:T(8,128)S(1)}, u32[]{:S(2)}, u32[]{:S(2)}) %collective-permute-start.6) | collective-permute-done | bytes 16416 | tf_op jit(solution)/shard_map/ppermute | solution.py:19
  31.9 1.9 %collective-permute-done.5 = f32[8,512]{1,0:T(8,128)S(1)} collective-permute-done((f32[8,512]{1,0:T(8,128)S(1)}, f32[8,512]{1,0:T(8,128)S(1)}, u32[]{:S(2)}, u32[]{:S(2)}) %collective-permute-start.5) | collective-permute-done | bytes 16416 | tf_op jit(solution)/shard_map/ppermute | solution.py:17
  40.3 9.8 %all-gather = bf16[384,512]{1,0:T(8,128)(2,1)S(1)} all-gather(bf16[48,512]{1,0:T(8,128)(2,1)S(1)} %fusion.1), channel_id=2, replica_groups=mesh['tm'=8,'space'=4] {'tm'}, dimensions={0}, use_global_device_ids=true | all-gather | bytes 442368 | tf_op jit(solution)/shard_map/all_gather | solution.py:79
  51.1 10.0 %while.20 = (s32[]{:T(128)}, f32[48,512]{1,0:T(8,128)S(1)}, s32[]{:T(128)}, f32[512,512]{1,0:T(8,128)S(1)}, f32[8,48,512]{2,1,0:T(8,128)}, /*index=5*/s32[]{:T(128)}, s32[]{:T(128)}, s32[]{:T(128)}) while((s32[]{:T(128)}, f32[48,512]{1,0:T(8,128)S(1)}, s32[]{:T(128)}, f32[512,512]{1,0:T(8,128)S(1)}, f32[8,48,512]{2,1,0:T(8,128)}, ...), condition=%wide.region_1.2_spmd, body=%wide.region_0.1_spmd.sunk | while | flops 151019520 | bytes 1540227 | solution.py:86
  62.0 3.9 %collective-permute-start.7 = (f32[48,512]{1,0:T(8,128)S(1)}, f32[48,512]{1,0:T(8,128)S(1)}, u32[]{:S(2)}, u32[]{:S(2)}) collective-permute-start(f32[48,512]{1,0:T(8,128)S(1)} %add.433), channel_id=1, source_target_pairs={{0,4},{4,8},{8,12},{12,16},{16,20},{20,24},{24,28},{1,5},{5,9},{9,... | collective-permute-start | bytes 294920 | tf_op jit(solution)/shard_map/ppermute | solution.py:29
  66.0 2.0 %collective-permute-done.7 = f32[48,512]{1,0:T(8,128)S(1)} collective-permute-done((f32[48,512]{1,0:T(8,128)S(1)}, f32[48,512]{1,0:T(8,128)S(1)}, u32[]{:S(2)}, u32[]{:S(2)}) %collective-permute-start.7) | collective-permute-done | bytes 98336 | tf_op jit(solution)/shard_map/ppermute | solution.py:29
  68.1 2.0 %collective-permute-start.8 = (f32[8,512]{1,0:T(8,128)S(1)}, f32[8,512]{1,0:T(8,128)S(1)}, u32[]{:S(2)}, u32[]{:S(2)}) collective-permute-start(f32[8,512]{1,0:T(8,128)S(1)} %get-tuple-element.97), channel_id=1, source_target_pairs={{0,1},{1,2},{2,3},{3,0},{4,5},{5,6},{6,7},{7,4},{8,9},{9,10},{10,1... | collective-permute-start | bytes 49160 | tf_op jit(solution)/shard_map/ppermute | solution.py:17
  71.8 1.9 %collective-permute-done.8 = f32[8,512]{1,0:T(8,128)S(1)} collective-permute-done((f32[8,512]{1,0:T(8,128)S(1)}, f32[8,512]{1,0:T(8,128)S(1)}, u32[]{:S(2)}, u32[]{:S(2)}) %collective-permute-start.8) | collective-permute-done | bytes 16416 | tf_op jit(solution)/shard_map/ppermute | solution.py:17
  80.2 1.9 %collective-permute-start.10 = (f32[48,512]{1,0:T(8,128)S(1)}, f32[48,512]{1,0:T(8,128)S(1)}, u32[]{:S(2)}, u32[]{:S(2)}) collective-permute-start(f32[48,512]{1,0:T(8,128)S(1)} %fusion.183), channel_id=1, source_target_pairs={{0,4},{4,8},{8,12},{12,16},{16,20},{20,24},{24,28},{1,5},{5,9},{9,... | collective-permute-start | bytes 294920 | tf_op jit(solution)/shard_map/ppermute | solution.py:29
  82.1 4.0 %collective-permute-done.10 = f32[48,512]{1,0:T(8,128)S(1)} collective-permute-done((f32[48,512]{1,0:T(8,128)S(1)}, f32[48,512]{1,0:T(8,128)S(1)}, u32[]{:S(2)}, u32[]{:S(2)}) %collective-permute-start.10) | collective-permute-done | bytes 98336 | tf_op jit(solution)/shard_map/ppermute | solution.py:29
  87.5 2.0 %collective-permute-start.11 = (f32[8,512]{1,0:T(8,128)S(1)}, f32[8,512]{1,0:T(8,128)S(1)}, u32[]{:S(2)}, u32[]{:S(2)}) collective-permute-start(f32[8,512]{1,0:T(8,128)S(1)} %get-tuple-element.95), channel_id=1, source_target_pairs={{0,1},{1,2},{2,3},{3,0},{4,5},{5,6},{6,7},{7,4},{8,9},{9,10},{10,1... | collective-permute-start | bytes 49160 | tf_op jit(solution)/shard_map/ppermute | solution.py:17
  89.4 1.9 %collective-permute-done.12 = f32[8,512]{1,0:T(8,128)S(1)} collective-permute-done((f32[8,512]{1,0:T(8,128)}, f32[8,512]{1,0:T(8,128)S(1)}, u32[]{:S(2)}, u32[]{:S(2)}) %collective-permute-start.12) | collective-permute-done | bytes 16416 | tf_op jit(solution)/shard_map/ppermute | solution.py:19
  100.4 8.4 %all-gather.1 = bf16[384,512]{1,0:T(8,128)(2,1)S(1)} all-gather(bf16[48,512]{1,0:T(8,128)(2,1)S(1)} %fusion.2), channel_id=3, replica_groups=mesh['tm'=8,'space'=4] {'tm'}, dimensions={0}, use_global_device_ids=true | all-gather | bytes 442368 | tf_op jit(solution)/shard_map/all_gather | solution.py:79
  109.7 10.0 %while.21 = (s32[]{:T(128)}, f32[48,512]{1,0:T(8,128)S(1)}, s32[]{:T(128)}, f32[512,512]{1,0:T(8,128)S(1)}, f32[8,48,512]{2,1,0:T(8,128)}, /*index=5*/s32[]{:T(128)}, s32[]{:T(128)}, s32[]{:T(128)}) while((s32[]{:T(128)}, f32[48,512]{1,0:T(8,128)S(1)}, s32[]{:T(128)}, f32[512,512]{1,0:T(8,128)S(1)}, f32[8,48,512]{2,1,0:T(8,128)}, ...), condition=%wide.region_3.4_spmd, body=%wide.region_2.3_spmd.sunk | while | flops 151019520 | bytes 1540227 | solution.py:86
  119.7 3.9 %collective-permute-start.13 = (f32[48,512]{1,0:T(8,128)S(1)}, f32[48,512]{1,0:T(8,128)S(1)}, u32[]{:S(2)}, u32[]{:S(2)}) collective-permute-start(f32[48,512]{1,0:T(8,128)S(1)} %add.482), channel_id=1, source_target_pairs={{0,4},{4,8},{8,12},{12,16},{16,20},{20,24},{24,28},{1,5},{5,9},{9,... | collective-permute-start | bytes 294920 | tf_op jit(solution)/shard_map/ppermute | solution.py:29
  123.7 2.0 %collective-permute-done.13 = f32[48,512]{1,0:T(8,128)S(1)} collective-permute-done((f32[48,512]{1,0:T(8,128)S(1)}, f32[48,512]{1,0:T(8,128)S(1)}, u32[]{:S(2)}, u32[]{:S(2)}) %collective-permute-start.13) | collective-permute-done | bytes 98336 | tf_op jit(solution)/shard_map/ppermute | solution.py:29
  126.0 1.8 %collective-permute-start.14 = (f32[8,512]{1,0:T(8,128)S(1)}, f32[8,512]{1,0:T(8,128)S(1)}, u32[]{:S(2)}, u32[]{:S(2)}) collective-permute-start(f32[8,512]{1,0:T(8,128)S(1)} %get-tuple-element.93), channel_id=1, source_target_pairs={{0,1},{1,2},{2,3},{3,0},{4,5},{5,6},{6,7},{7,4},{8,9},{9,10},{10,1... | collective-permute-start | bytes 49160 | tf_op jit(solution)/shard_map/ppermute | solution.py:17
  129.5 2.0 %collective-permute-done.14 = f32[8,512]{1,0:T(8,128)S(1)} collective-permute-done((f32[8,512]{1,0:T(8,128)S(1)}, f32[8,512]{1,0:T(8,128)S(1)}, u32[]{:S(2)}, u32[]{:S(2)}) %collective-permute-start.14) | collective-permute-done | bytes 16416 | tf_op jit(solution)/shard_map/ppermute | solution.py:17
  (140 shorter events, 68.1 us)
Async XLA Ops:
  0.0 14.9 %copy-start = (f32[512,512]{1,0:T(8,128)S(1)}, f32[512,512]{1,0:T(8,128)}, u32[]{:S(2)}) copy-start(f32[512,512]{1,0:T(8,128)} %param.14) | copy-start | bytes 3145732
  0.0 3.7 %copy-start.4 = (bf16[48,512]{1,0:T(8,128)(2,1)S(1)}, bf16[48,512]{1,0:T(8,128)(2,1)}, u32[]{:S(2)}) copy-start(bf16[48,512]{1,0:T(8,128)(2,1)} %param.11) | copy-start | bytes 147460
  0.0 3.7 %copy-start.3 = (bf16[48,512]{1,0:T(8,128)(2,1)S(1)}, bf16[48,512]{1,0:T(8,128)(2,1)}, u32[]{:S(2)}) copy-start(bf16[48,512]{1,0:T(8,128)(2,1)} %param.12) | copy-start | bytes 147460
  0.1 8.5 %collective-permute-start.3 = (f32[8,512]{1,0:T(8,128)S(1)}, f32[8,512]{1,0:T(8,128)S(1)}, u32[]{:S(2)}, u32[]{:S(2)}) collective-permute-start(f32[8,512]{1,0:T(8,128)S(1)} %get-tuple-element.102), channel_id=1, source_target_pairs={{1,0},{2,1},{3,2},{0,3},{5,4},{6,5},{7,6},{4,7},{9,8},{10,9},{11,1... | collective-permute-start | bytes 49160 | tf_op jit(solution)/shard_map/ppermute | solution.py:19
  3.7 5.7 %collective-permute-start.2 = (f32[8,512]{1,0:T(8,128)S(1)}, f32[8,512]{1,0:T(8,128)S(1)}, u32[]{:S(2)}, u32[]{:S(2)}) collective-permute-start(f32[8,512]{1,0:T(8,128)S(1)} %get-tuple-element.101), channel_id=1, source_target_pairs={{0,1},{1,2},{2,3},{3,0},{4,5},{5,6},{6,7},{7,4},{8,9},{9,10},{10,1... | collective-permute-start | bytes 49160 | tf_op jit(solution)/shard_map/ppermute | solution.py:17
  3.7 11.1 %copy-start.2 = (bf16[8,48,512]{2,1,0:T(8,128)(2,1)S(1)}, bf16[8,48,512]{2,1,0:T(8,128)(2,1)}, u32[]{:S(2)}) copy-start(bf16[8,48,512]{2,1,0:T(8,128)(2,1)} %param.13) | copy-start | bytes 1179652
  4.7 5.9 %collective-permute-start.1 = (bf16[10,8,512]{2,1,0:T(8,128)(2,1)S(1)}, bf16[10,8,512]{2,1,0:T(8,128)(2,1)S(1)}, u32[]{:S(2)}, u32[]{:S(2)}) collective-permute-start(bf16[10,8,512]{2,1,0:T(8,128)(2,1)S(1)} %get-tuple-element.89), channel_id=1, source_target_pairs={{1,0},{2,1},{3,2},{0,3},{5,4},{6,5},{7,6},{4,7},{9,8},{10,9},{11,1... | collective-permute-start | bytes 245768 | tf_op jit(solution)/shard_map/ppermute | solution.py:19
  8.5 6.2 %collective-permute-start = (bf16[10,8,512]{2,1,0:T(8,128)(2,1)S(1)}, bf16[10,8,512]{2,1,0:T(8,128)(2,1)S(1)}, u32[]{:S(2)}, u32[]{:S(2)}) collective-permute-start(bf16[10,8,512]{2,1,0:T(8,128)(2,1)S(1)} %get-tuple-element.88), channel_id=1, source_target_pairs={{0,1},{1,2},{2,3},{3,0},{4,5},{5,6},{6,7},{7,4},{8,9},{9,10},{10,1... | collective-permute-start | bytes 245768 | tf_op jit(solution)/shard_map/ppermute | solution.py:17
  20.6 18.2 %copy-start.6 = (bf16[50,512]{1,0:T(8,128)(2,1)}, bf16[50,512]{1,0:T(8,128)(2,1)S(1)}, u32[]{:S(2)}) copy-start(bf16[50,512]{1,0:T(8,128)(2,1)S(1)} %get-tuple-element.84) | copy-start | bytes 153604
  21.4 6.7 %copy-start.5 = (f32[48,512]{1,0:T(8,128)S(1)}, f32[48,512]{1,0:T(8,128)}, u32[]{:S(2)}) copy-start(f32[48,512]{1,0:T(8,128)} %param.10) | copy-start | bytes 294916
  22.2 17.4 %copy-start.8 = (f32[48,512]{1,0:T(8,128)}, f32[48,512]{1,0:T(8,128)S(1)}, u32[]{:S(2)}) copy-start(f32[48,512]{1,0:T(8,128)S(1)} %fusion.182) | copy-start | bytes 294916
  22.2 5.9 %collective-permute-start.4 = (f32[48,512]{1,0:T(8,128)S(1)}, f32[48,512]{1,0:T(8,128)S(1)}, u32[]{:S(2)}, u32[]{:S(2)}) collective-permute-start(f32[48,512]{1,0:T(8,128)S(1)} %fusion.182), channel_id=1, source_target_pairs={{0,4},{4,8},{8,12},{12,16},{16,20},{20,24},{24,28},{1,5},{5,9},{9,... | collective-permute-start | bytes 294920 | tf_op jit(solution)/shard_map/ppermute | solution.py:29
  28.2 3.8 %collective-permute-start.6 = (f32[8,512]{1,0:T(8,128)S(1)}, f32[8,512]{1,0:T(8,128)S(1)}, u32[]{:S(2)}, u32[]{:S(2)}) collective-permute-start(f32[8,512]{1,0:T(8,128)S(1)} %get-tuple-element.100), channel_id=1, source_target_pairs={{1,0},{2,1},{3,2},{0,3},{5,4},{6,5},{7,6},{4,7},{9,8},{10,9},{11,1... | collective-permute-start | bytes 49160 | tf_op jit(solution)/shard_map/ppermute | solution.py:19
  28.3 5.5 %collective-permute-start.5 = (f32[8,512]{1,0:T(8,128)S(1)}, f32[8,512]{1,0:T(8,128)S(1)}, u32[]{:S(2)}, u32[]{:S(2)}) collective-permute-start(f32[8,512]{1,0:T(8,128)S(1)} %get-tuple-element.99), channel_id=1, source_target_pairs={{0,1},{1,2},{2,3},{3,0},{4,5},{5,6},{6,7},{7,4},{8,9},{9,10},{10,1... | collective-permute-start | bytes 49160 | tf_op jit(solution)/shard_map/ppermute | solution.py:17
  40.3 10.8 %copy-start.1 = (f32[512,512]{1,0:T(8,128)S(1)}, f32[512,512]{1,0:T(8,128)}, u32[]{:S(2)}) copy-start(f32[512,512]{1,0:T(8,128)} %param.15) | copy-start | bytes 3145732
  62.0 5.9 %collective-permute-start.7 = (f32[48,512]{1,0:T(8,128)S(1)}, f32[48,512]{1,0:T(8,128)S(1)}, u32[]{:S(2)}, u32[]{:S(2)}) collective-permute-start(f32[48,512]{1,0:T(8,128)S(1)} %add.433), channel_id=1, source_target_pairs={{0,4},{4,8},{8,12},{12,16},{16,20},{20,24},{24,28},{1,5},{5,9},{9,... | collective-permute-start | bytes 294920 | tf_op jit(solution)/shard_map/ppermute | solution.py:29
  68.0 3.8 %collective-permute-start.9 = (f32[8,512]{1,0:T(8,128)S(1)}, f32[8,512]{1,0:T(8,128)S(1)}, u32[]{:S(2)}, u32[]{:S(2)}) collective-permute-start(f32[8,512]{1,0:T(8,128)S(1)} %get-tuple-element.98), channel_id=1, source_target_pairs={{1,0},{2,1},{3,2},{0,3},{5,4},{6,5},{7,6},{4,7},{9,8},{10,9},{11,1... | collective-permute-start | bytes 49160 | tf_op jit(solution)/shard_map/ppermute | solution.py:19
  68.1 5.6 %collective-permute-start.8 = (f32[8,512]{1,0:T(8,128)S(1)}, f32[8,512]{1,0:T(8,128)S(1)}, u32[]{:S(2)}, u32[]{:S(2)}) collective-permute-start(f32[8,512]{1,0:T(8,128)S(1)} %get-tuple-element.97), channel_id=1, source_target_pairs={{0,1},{1,2},{2,3},{3,0},{4,5},{5,6},{6,7},{7,4},{8,9},{9,10},{10,1... | collective-permute-start | bytes 49160 | tf_op jit(solution)/shard_map/ppermute | solution.py:17
  80.2 5.9 %collective-permute-start.10 = (f32[48,512]{1,0:T(8,128)S(1)}, f32[48,512]{1,0:T(8,128)S(1)}, u32[]{:S(2)}, u32[]{:S(2)}) collective-permute-start(f32[48,512]{1,0:T(8,128)S(1)} %fusion.183), channel_id=1, source_target_pairs={{0,4},{4,8},{8,12},{12,16},{16,20},{20,24},{24,28},{1,5},{5,9},{9,... | collective-permute-start | bytes 294920 | tf_op jit(solution)/shard_map/ppermute | solution.py:29
  87.4 3.9 %collective-permute-start.12 = (f32[8,512]{1,0:T(8,128)}, f32[8,512]{1,0:T(8,128)S(1)}, u32[]{:S(2)}, u32[]{:S(2)}) collective-permute-start(f32[8,512]{1,0:T(8,128)} %get-tuple-element.96), channel_id=1, source_target_pairs={{1,0},{2,1},{3,2},{0,3},{5,4},{6,5},{7,6},{4,7},{9,8},{10,9},{11,1... | collective-permute-start | bytes 49160 | tf_op jit(solution)/shard_map/ppermute | solution.py:19
  87.5 5.5 %collective-permute-start.11 = (f32[8,512]{1,0:T(8,128)S(1)}, f32[8,512]{1,0:T(8,128)S(1)}, u32[]{:S(2)}, u32[]{:S(2)}) collective-permute-start(f32[8,512]{1,0:T(8,128)S(1)} %get-tuple-element.95), channel_id=1, source_target_pairs={{0,1},{1,2},{2,3},{3,0},{4,5},{5,6},{6,7},{7,4},{8,9},{9,10},{10,1... | collective-permute-start | bytes 49160 | tf_op jit(solution)/shard_map/ppermute | solution.py:17
  119.7 5.9 %collective-permute-start.13 = (f32[48,512]{1,0:T(8,128)S(1)}, f32[48,512]{1,0:T(8,128)S(1)}, u32[]{:S(2)}, u32[]{:S(2)}) collective-permute-start(f32[48,512]{1,0:T(8,128)S(1)} %add.482), channel_id=1, source_target_pairs={{0,4},{4,8},{8,12},{12,16},{16,20},{20,24},{24,28},{1,5},{5,9},{9,... | collective-permute-start | bytes 294920 | tf_op jit(solution)/shard_map/ppermute | solution.py:29
  125.7 3.8 %collective-permute-start.15 = (f32[8,512]{1,0:T(8,128)S(1)}, f32[8,512]{1,0:T(8,128)S(1)}, u32[]{:S(2)}, u32[]{:S(2)}) collective-permute-start(f32[8,512]{1,0:T(8,128)S(1)} %get-tuple-element.94), channel_id=1, source_target_pairs={{1,0},{2,1},{3,2},{0,3},{5,4},{6,5},{7,6},{4,7},{9,8},{10,9},{11,1... | collective-permute-start | bytes 49160 | tf_op jit(solution)/shard_map/ppermute | solution.py:19
  126.0 5.5 %collective-permute-start.14 = (f32[8,512]{1,0:T(8,128)S(1)}, f32[8,512]{1,0:T(8,128)S(1)}, u32[]{:S(2)}, u32[]{:S(2)}) collective-permute-start(f32[8,512]{1,0:T(8,128)S(1)} %get-tuple-element.93), channel_id=1, source_target_pairs={{0,1},{1,2},{2,3},{3,0},{4,5},{5,6},{6,7},{7,4},{8,9},{9,10},{10,1... | collective-permute-start | bytes 49160 | tf_op jit(solution)/shard_map/ppermute | solution.py:17
  (4 other events, 3.2 us)
where the time goes:
time: 141 us; the launch traced here: 140 us
  matrix products  50.9 us (36%)
  waiting for transfers between devices  32.7 us (23%)
  starting transfers between devices  27.5 us (20%)
  blocking collectives  18.2 us (13%)
  other arithmetic  5.67 us (4%)
  local copies, waits for them, and re-layouts  3.93 us (3%)
    dot_general x51, matrix products, apply_matrix(): jnp.dot(field, matrix, precision=HIGHEST, preferred_element_type=jnp.floa...  50.9 us
    all_gather x2, blocking collectives, per_device(): lax.all_gather(residual[None].astype(jnp.bfloat16), 'tm', axis=0, tiled=T...  18.2 us
    ppermute x6, waiting for transfers between devices, with_halo(): lax.ppermute(tail, axis, [(i, (i + 1) % count) for i in range(count)])  12.5 us
    ppermute x4, waiting for transfers between devices, from_behind(): return lax.ppermute(block, axis, route)  12 us
    ppermute x4, starting transfers between devices, from_behind(): return lax.ppermute(block, axis, route)  11.7 us
    ppermute x6, waiting for transfers between devices, with_halo(): lax.ppermute(head, axis, [((i + 1) % count, i) for i in range(count)])  8.21 us
    ppermute x6, starting transfers between devices, with_halo(): lax.ppermute(head, axis, [((i + 1) % count, i) for i in range(count)])  8.03 us
    ppermute x6, starting transfers between devices, with_halo(): lax.ppermute(tail, axis, [(i, (i + 1) % count) for i in range(count)])  7.74 us
  transfers between devices with their start and end apart: 16, of which 15 were waited for; matrix products, arithmetic and copies ran while one was open for 1% of the time, Pallas kernels for 0%

commit v1 on v0

--- a/solution.py
+++ b/solution.py
@@ -5,6 +5,27 @@
 
 CYCLES = 2
 HIGHEST = lax.Precision.HIGHEST
+
+
+def ring_gather(x, axis, dim):
+    size, here, span = (lax.axis_size(axis), lax.axis_index(axis), x.shape[dim])
+    forward = [(i, (i + 1) % size) for i in range(size)]
+    left = [(i, (i - 1) % size) for i in range(size)]
+    whole = jnp.zeros((*x.shape[:dim], size * span, *x.shape[dim + 1 :]), x.dtype)
+    whole = lax.dynamic_update_slice_in_dim(whole, x, here * span, axis=dim)
+    from_left = from_right = x
+    halfway = size // 2
+    for step in range(1, halfway + 1):
+        from_left = lax.ppermute(from_left, axis, forward)
+        whole = lax.dynamic_update_slice_in_dim(
+            whole, from_left, (here - step) % size * span, axis=dim
+        )
+        if step < size - halfway:
+            from_right = lax.ppermute(from_right, axis, left)
+            whole = lax.dynamic_update_slice_in_dim(
+                whole, from_right, (here + step) % size * span, axis=dim
+            )
+    return whole
 
 
 def with_halo(cells, sides, width):
@@ -76,9 +97,7 @@
             begin_state = previous(end_values)
         end_values = relax_block(begin_state, block_steps)[-1]
         residual = relax_block(previous(end_values), block_steps)[-1] - end_values
-        gathered = lax.all_gather(
-            residual[None].astype(jnp.bfloat16), "tm", axis=0, tiled=True
-        ).astype(jnp.float32)
+        gathered = ring_gather(residual[None].astype(jnp.bfloat16), "tm", 0).astype(jnp.float32)
 
         def coarse_turn(source, carried):
             return apply_matrix(carried, coarse_implicit) + gathered[source]

time: 141 us -> 158 us (1.12)
  the two profiles are of different devices: /device:TPU:6 before, /device:TPU:4 now
where the time goes in v1:
time: 158 us
  waiting for transfers between devices  52.6 us (33%)
  matrix products  45 us (28%)
  starting transfers between devices  39.5 us (25%)
  local copies, waits for them, and re-layouts  14.7 us (9%)
  other arithmetic  5 us (3%)
    dot_general x47, matrix products, apply_matrix(): jnp.dot(field, matrix, precision=HIGHEST, preferred_element_type=jnp.floa...  45 us
    ppermute x4, waiting for transfers between devices, from_behind(): return lax.ppermute(block, axis, route)  19.6 us
    ppermute x6, starting transfers between devices, ring_gather(): from_right = lax.ppermute(from_right, axis, left)  16 us
    ppermute x6, waiting for transfers between devices, with_halo(): lax.ppermute(tail, axis, [(i, (i + 1) % count) for i in range(count)])  12.7 us
    ppermute x8, waiting for transfers between devices, ring_gather(): from_left = lax.ppermute(from_left, axis, forward)  12.2 us
    ppermute x6, waiting for transfers between devices, with_halo(): lax.ppermute(head, axis, [((i + 1) % count, i) for i in range(count)])  8 us
    ppermute x6, starting transfers between devices, with_halo(): lax.ppermute(tail, axis, [(i, (i + 1) % count) for i in range(count)])  7.97 us
    ppermute x6, starting transfers between devices, with_halo(): lax.ppermute(head, axis, [((i + 1) % count, i) for i in range(count)])  7.85 us
  transfers between devices with their start and end apart: 30, of which 23 were waited for; matrix products, arithmetic and copies ran while one was open for 5% of the time, Pallas kernels for 0%

profile of v1, /device:TPU:4, one launch (start us, length us, event | category | flops | bytes accessed | tf_op | source)
XLA Modules:
  0.0 157.7 jit_solution(7131737472137469353)
XLA Ops:
  0.1 3.7 %collective-permute-start.3 = (f32[8,512]{1,0:T(8,128)S(1)}, f32[8,512]{1,0:T(8,128)S(1)}, u32[]{:S(2)}, u32[]{:S(2)}) collective-permute-start(f32[8,512]{1,0:T(8,128)S(1)} %get-tuple-element.102), channel_id=1, source_target_pairs={{1,0},{2,1},{3,2},{0,3},{5,4},{6,5},{7,6},{4,7},{9,8},{10,9},{11,1... | collective-permute-start | bytes 49160 | tf_op jit(solution)/shard_map/ppermute | solution.py:40
  4.7 3.9 %collective-permute-start.1 = (bf16[10,8,512]{2,1,0:T(8,128)(2,1)S(1)}, bf16[10,8,512]{2,1,0:T(8,128)(2,1)S(1)}, u32[]{:S(2)}, u32[]{:S(2)}) collective-permute-start(bf16[10,8,512]{2,1,0:T(8,128)(2,1)S(1)} %get-tuple-element.89), channel_id=1, source_target_pairs={{1,0},{2,1},{3,2},{0,3},{5,4},{6,5},{7,6},{4,7},{9,8},{10,9},{11,1... | collective-permute-start | bytes 245768 | tf_op jit(solution)/shard_map/ppermute | solution.py:40
  10.6 4.2 %collective-permute-done = bf16[10,8,512]{2,1,0:T(8,128)(2,1)S(1)} collective-permute-done((bf16[10,8,512]{2,1,0:T(8,128)(2,1)S(1)}, bf16[10,8,512]{2,1,0:T(8,128)(2,1)S(1)}, u32[]{:S(2)}, u32[]{:S(2)}) %collective-permute-start) | collective-permute-done | bytes 81952 | tf_op jit(solution)/shard_map/ppermute | solution.py:38
  24.1 4.9 %collective-permute-done.4 = f32[48,512]{1,0:T(8,128)S(1)} collective-permute-done((f32[48,512]{1,0:T(8,128)S(1)}, f32[48,512]{1,0:T(8,128)S(1)}, u32[]{:S(2)}, u32[]{:S(2)}) %collective-permute-start.4) | collective-permute-done | bytes 98336 | tf_op jit(solution)/shard_map/ppermute | solution.py:50
  29.2 2.0 %collective-permute-start.5 = (f32[8,512]{1,0:T(8,128)S(1)}, f32[8,512]{1,0:T(8,128)S(1)}, u32[]{:S(2)}, u32[]{:S(2)}) collective-permute-start(f32[8,512]{1,0:T(8,128)S(1)} %get-tuple-element.99), channel_id=1, source_target_pairs={{0,1},{1,2},{2,3},{3,0},{4,5},{5,6},{6,7},{7,4},{8,9},{9,10},{10,1... | collective-permute-start | bytes 49160 | tf_op jit(solution)/shard_map/ppermute | solution.py:38
  42.6 2.6 %collective-permute-start.8 = (bf16[1,48,512]{2,1,0:T(8,128)(2,1)S(1)}, bf16[1,48,512]{2,1,0:T(8,128)(2,1)S(1)}, u32[]{:S(2)}, u32[]{:S(2)}) collective-permute-start(bf16[1,48,512]{2,1,0:T(8,128)(2,1)S(1)} %get-tuple-element.106), channel_id=1, source_target_pairs={{0,28},{4,0},{8,4},{12,8},{16,12},{20,16},{24,20},{28,24},{1,29},{... | collective-permute-start | bytes 147464 | tf_op jit(solution)/shard_map/ppermute | solution.py:24
  45.3 2.2 %collective-permute-done.7 = bf16[1,48,512]{2,1,0:T(8,128)(2,1)S(1)} collective-permute-done((bf16[1,48,512]{2,1,0:T(8,128)(2,1)S(1)}, bf16[1,48,512]{2,1,0:T(8,128)(2,1)S(1)}, u32[]{:S(2)}, u32[]{:S(2)}) %collective-permute-start.7) | collective-permute-done | bytes 49184 | tf_op jit(solution)/shard_map/ppermute | solution.py:19
  47.5 2.6 %collective-permute-start.10 = (bf16[1,48,512]{2,1,0:T(8,128)(2,1)S(1)}, bf16[1,48,512]{2,1,0:T(8,128)(2,1)S(1)}, u32[]{:S(2)}, u32[]{:S(2)}) collective-permute-start(bf16[1,48,512]{2,1,0:T(8,128)(2,1)S(1)} %collective-permute-done.8), channel_id=1, source_target_pairs={{0,28},{4,0},{8,4},{12,8},{16,12},{20,16},{24,20},{28,24},{1,29},{... | collective-permute-start | bytes 147464 | tf_op jit(solution)/shard_map/ppermute | solution.py:24
  52.0 2.8 %collective-permute-start.12 = (bf16[1,48,512]{2,1,0:T(8,128)(2,1)S(1)}, bf16[1,48,512]{2,1,0:T(8,128)(2,1)S(1)}, u32[]{:S(2)}, u32[]{:S(2)}) collective-permute-start(bf16[1,48,512]{2,1,0:T(8,128)(2,1)S(1)} %collective-permute-done.10), channel_id=1, source_target_pairs={{0,28},{4,0},{8,4},{12,8},{16,12},{20,16},{24,20},{28,24},{1,29},{... | collective-permute-start | bytes 147464 | tf_op jit(solution)/shard_map/ppermute | solution.py:24
  57.6 3.2 %collective-permute-done.13 = bf16[1,48,512]{2,1,0:T(8,128)(2,1)S(1)} collective-permute-done((bf16[1,48,512]{2,1,0:T(8,128)(2,1)S(1)}, bf16[1,48,512]{2,1,0:T(8,128)(2,1)S(1)}, u32[]{:S(2)}, u32[]{:S(2)}) %collective-permute-start.13) | collective-permute-done | bytes 49184 | tf_op jit(solution)/shard_map/ppermute | solution.py:19
  63.4 6.6 %while.20 = (s32[]{:T(128)}, f32[48,512]{1,0:T(8,128)S(1)}, s32[]{:T(128)}, f32[512,512]{1,0:T(8,128)S(1)}, f32[8,48,512]{2,1,0:T(8,128)}, /*index=5*/s32[]{:T(128)}, s32[]{:T(128)}, s32[]{:T(128)}) while((s32[]{:T(128)}, f32[48,512]{1,0:T(8,128)S(1)}, s32[]{:T(128)}, f32[512,512]{1,0:T(8,128)S(1)}, f32[8,48,512]{2,1,0:T(8,128)}, ...), condition=%wide.region_1.2_spmd, body=%wide.region_0.1_spmd.sunk | while | flops 151019520 | bytes 1540227 | solution.py:105
  72.8 4.9 %collective-permute-done.14 = f32[48,512]{1,0:T(8,128)S(1)} collective-permute-done((f32[48,512]{1,0:T(8,128)S(1)}, f32[48,512]{1,0:T(8,128)S(1)}, u32[]{:S(2)}, u32[]{:S(2)}) %collective-permute-start.14) | collective-permute-done | bytes 98336 | tf_op jit(solution)/shard_map/ppermute | solution.py:50
  77.9 2.0 %collective-permute-start.15 = (f32[8,512]{1,0:T(8,128)S(1)}, f32[8,512]{1,0:T(8,128)S(1)}, u32[]{:S(2)}, u32[]{:S(2)}) collective-permute-start(f32[8,512]{1,0:T(8,128)S(1)} %get-tuple-element.97), channel_id=1, source_target_pairs={{0,1},{1,2},{2,3},{3,0},{4,5},{5,6},{6,7},{7,4},{8,9},{9,10},{10,1... | collective-permute-start | bytes 49160 | tf_op jit(solution)/shard_map/ppermute | solution.py:38
  90.0 1.9 %collective-permute-start.17 = (f32[48,512]{1,0:T(8,128)S(1)}, f32[48,512]{1,0:T(8,128)S(1)}, u32[]{:S(2)}, u32[]{:S(2)}) collective-permute-start(f32[48,512]{1,0:T(8,128)S(1)} %fusion.185), channel_id=1, source_target_pairs={{0,4},{4,8},{8,12},{12,16},{16,20},{20,24},{24,28},{1,5},{5,9},{9,... | collective-permute-start | bytes 294920 | tf_op jit(solution)/shard_map/ppermute | solution.py:50
  91.9 4.9 %collective-permute-done.17 = f32[48,512]{1,0:T(8,128)S(1)} collective-permute-done((f32[48,512]{1,0:T(8,128)S(1)}, f32[48,512]{1,0:T(8,128)S(1)}, u32[]{:S(2)}, u32[]{:S(2)}) %collective-permute-start.17) | collective-permute-done | bytes 98336 | tf_op jit(solution)/shard_map/ppermute | solution.py:50
  96.9 2.0 %collective-permute-start.18 = (f32[8,512]{1,0:T(8,128)S(1)}, f32[8,512]{1,0:T(8,128)S(1)}, u32[]{:S(2)}, u32[]{:S(2)}) collective-permute-start(f32[8,512]{1,0:T(8,128)S(1)} %get-tuple-element.95), channel_id=1, source_target_pairs={{0,1},{1,2},{2,3},{3,0},{4,5},{5,6},{6,7},{7,4},{8,9},{9,10},{10,1... | collective-permute-start | bytes 49160 | tf_op jit(solution)/shard_map/ppermute | solution.py:38
  100.6 2.1 %collective-permute-done.18 = f32[8,512]{1,0:T(8,128)S(1)} collective-permute-done((f32[8,512]{1,0:T(8,128)S(1)}, f32[8,512]{1,0:T(8,128)S(1)}, u32[]{:S(2)}, u32[]{:S(2)}) %collective-permute-start.18) | collective-permute-done | bytes 16416 | tf_op jit(solution)/shard_map/ppermute | solution.py:38
  110.0 2.6 %collective-permute-start.21 = (bf16[1,48,512]{2,1,0:T(8,128)(2,1)S(1)}, bf16[1,48,512]{2,1,0:T(8,128)(2,1)S(1)}, u32[]{:S(2)}, u32[]{:S(2)}) collective-permute-start(bf16[1,48,512]{2,1,0:T(8,128)(2,1)S(1)} %get-tuple-element.108), channel_id=1, source_target_pairs={{0,28},{4,0},{8,4},{12,8},{16,12},{20,16},{24,20},{28,24},{1,29},{... | collective-permute-start | bytes 147464 | tf_op jit(solution)/shard_map/ppermute | solution.py:24
  115.0 2.6 %collective-permute-start.23 = (bf16[1,48,512]{2,1,0:T(8,128)(2,1)S(1)}, bf16[1,48,512]{2,1,0:T(8,128)(2,1)S(1)}, u32[]{:S(2)}, u32[]{:S(2)}) collective-permute-start(bf16[1,48,512]{2,1,0:T(8,128)(2,1)S(1)} %collective-permute-done.21), channel_id=1, source_target_pairs={{0,28},{4,0},{8,4},{12,8},{16,12},{20,16},{24,20},{28,24},{1,29},{... | collective-permute-start | bytes 147464 | tf_op jit(solution)/shard_map/ppermute | solution.py:24
  119.5 2.6 %collective-permute-start.25 = (bf16[1,48,512]{2,1,0:T(8,128)(2,1)S(1)}, bf16[1,48,512]{2,1,0:T(8,128)(2,1)S(1)}, u32[]{:S(2)}, u32[]{:S(2)}) collective-permute-start(bf16[1,48,512]{2,1,0:T(8,128)(2,1)S(1)} %collective-permute-done.23), channel_id=1, source_target_pairs={{0,28},{4,0},{8,4},{12,8},{16,12},{20,16},{24,20},{28,24},{1,29},{... | collective-permute-start | bytes 147464 | tf_op jit(solution)/shard_map/ppermute | solution.py:24
  124.5 3.2 %collective-permute-done.26 = bf16[1,48,512]{2,1,0:T(8,128)(2,1)S(1)} collective-permute-done((bf16[1,48,512]{2,1,0:T(8,128)(2,1)S(1)}, bf16[1,48,512]{2,1,0:T(8,128)(2,1)S(1)}, u32[]{:S(2)}, u32[]{:S(2)}) %collective-permute-start.26) | collective-permute-done | bytes 49184 | tf_op jit(solution)/shard_map/ppermute | solution.py:19
  130.3 6.6 %while.21 = (s32[]{:T(128)}, f32[48,512]{1,0:T(8,128)S(1)}, s32[]{:T(128)}, f32[512,512]{1,0:T(8,128)S(1)}, f32[8,48,512]{2,1,0:T(8,128)}, /*index=5*/s32[]{:T(128)}, s32[]{:T(128)}, s32[]{:T(128)}) while((s32[]{:T(128)}, f32[48,512]{1,0:T(8,128)S(1)}, s32[]{:T(128)}, f32[512,512]{1,0:T(8,128)S(1)}, f32[8,48,512]{2,1,0:T(8,128)}, ...), condition=%wide.region_3.4_spmd, body=%wide.region_2.3_spmd.sunk | while | flops 151019520 | bytes 1540227 | solution.py:105
  138.9 4.9 %collective-permute-done.27 = f32[48,512]{1,0:T(8,128)S(1)} collective-permute-done((f32[48,512]{1,0:T(8,128)S(1)}, f32[48,512]{1,0:T(8,128)S(1)}, u32[]{:S(2)}, u32[]{:S(2)}) %collective-permute-start.27) | collective-permute-done | bytes 98336 | tf_op jit(solution)/shard_map/ppermute | solution.py:50
  143.9 2.0 %collective-permute-start.28 = (f32[8,512]{1,0:T(8,128)S(1)}, f32[8,512]{1,0:T(8,128)S(1)}, u32[]{:S(2)}, u32[]{:S(2)}) collective-permute-start(f32[8,512]{1,0:T(8,128)S(1)} %get-tuple-element.93), channel_id=1, source_target_pairs={{0,1},{1,2},{2,3},{3,0},{4,5},{5,6},{6,7},{7,4},{8,9},{9,10},{10,1... | collective-permute-start | bytes 49160 | tf_op jit(solution)/shard_map/ppermute | solution.py:38
  (178 shorter events, 89.0 us)
Async XLA Ops:
  0.1 8.5 %collective-permute-start.3 = (f32[8,512]{1,0:T(8,128)S(1)}, f32[8,512]{1,0:T(8,128)S(1)}, u32[]{:S(2)}, u32[]{:S(2)}) collective-permute-start(f32[8,512]{1,0:T(8,128)S(1)} %get-tuple-element.102), channel_id=1, source_target_pairs={{1,0},{2,1},{3,2},{0,3},{5,4},{6,5},{7,6},{4,7},{9,8},{10,9},{11,1... | collective-permute-start | bytes 49160 | tf_op jit(solution)/shard_map/ppermute | solution.py:40
  3.7 5.7 %collective-permute-start.2 = (f32[8,512]{1,0:T(8,128)S(1)}, f32[8,512]{1,0:T(8,128)S(1)}, u32[]{:S(2)}, u32[]{:S(2)}) collective-permute-start(f32[8,512]{1,0:T(8,128)S(1)} %get-tuple-element.101), channel_id=1, source_target_pairs={{0,1},{1,2},{2,3},{3,0},{4,5},{5,6},{6,7},{7,4},{8,9},{9,10},{10,1... | collective-permute-start | bytes 49160 | tf_op jit(solution)/shard_map/ppermute | solution.py:38
  4.7 5.9 %collective-permute-start.1 = (bf16[10,8,512]{2,1,0:T(8,128)(2,1)S(1)}, bf16[10,8,512]{2,1,0:T(8,128)(2,1)S(1)}, u32[]{:S(2)}, u32[]{:S(2)}) collective-permute-start(bf16[10,8,512]{2,1,0:T(8,128)(2,1)S(1)} %get-tuple-element.89), channel_id=1, source_target_pairs={{1,0},{2,1},{3,2},{0,3},{5,4},{6,5},{7,6},{4,7},{9,8},{10,9},{11,1... | collective-permute-start | bytes 245768 | tf_op jit(solution)/shard_map/ppermute | solution.py:40
  8.5 6.2 %collective-permute-start = (bf16[10,8,512]{2,1,0:T(8,128)(2,1)S(1)}, bf16[10,8,512]{2,1,0:T(8,128)(2,1)S(1)}, u32[]{:S(2)}, u32[]{:S(2)}) collective-permute-start(bf16[10,8,512]{2,1,0:T(8,128)(2,1)S(1)} %get-tuple-element.88), channel_id=1, source_target_pairs={{0,1},{1,2},{2,3},{3,0},{4,5},{5,6},{6,7},{7,4},{8,9},{9,10},{10,1... | collective-permute-start | bytes 245768 | tf_op jit(solution)/shard_map/ppermute | solution.py:38
  22.2 6.8 %collective-permute-start.4 = (f32[48,512]{1,0:T(8,128)S(1)}, f32[48,512]{1,0:T(8,128)S(1)}, u32[]{:S(2)}, u32[]{:S(2)}) collective-permute-start(f32[48,512]{1,0:T(8,128)S(1)} %fusion.184), channel_id=1, source_target_pairs={{0,4},{4,8},{8,12},{12,16},{16,20},{20,24},{24,28},{1,5},{5,9},{9,... | collective-permute-start | bytes 294920 | tf_op jit(solution)/shard_map/ppermute | solution.py:50
  29.2 5.5 %collective-permute-start.5 = (f32[8,512]{1,0:T(8,128)S(1)}, f32[8,512]{1,0:T(8,128)S(1)}, u32[]{:S(2)}, u32[]{:S(2)}) collective-permute-start(f32[8,512]{1,0:T(8,128)S(1)} %get-tuple-element.99), channel_id=1, source_target_pairs={{0,1},{1,2},{2,3},{3,0},{4,5},{5,6},{6,7},{7,4},{8,9},{9,10},{10,1... | collective-permute-start | bytes 49160 | tf_op jit(solution)/shard_map/ppermute | solution.py:38
  42.6 4.9 %collective-permute-start.7 = (bf16[1,48,512]{2,1,0:T(8,128)(2,1)S(1)}, bf16[1,48,512]{2,1,0:T(8,128)(2,1)S(1)}, u32[]{:S(2)}, u32[]{:S(2)}) collective-permute-start(bf16[1,48,512]{2,1,0:T(8,128)(2,1)S(1)} %get-tuple-element.106), channel_id=1, source_target_pairs={{0,4},{4,8},{8,12},{12,16},{16,20},{20,24},{24,28},{28,0},{1,5},{5... | collective-permute-start | bytes 147464 | tf_op jit(solution)/shard_map/ppermute | solution.py:19
  42.6 4.9 %collective-permute-start.8 = (bf16[1,48,512]{2,1,0:T(8,128)(2,1)S(1)}, bf16[1,48,512]{2,1,0:T(8,128)(2,1)S(1)}, u32[]{:S(2)}, u32[]{:S(2)}) collective-permute-start(bf16[1,48,512]{2,1,0:T(8,128)(2,1)S(1)} %get-tuple-element.106), channel_id=1, source_target_pairs={{0,28},{4,0},{8,4},{12,8},{16,12},{20,16},{24,20},{28,24},{1,29},{... | collective-permute-start | bytes 147464 | tf_op jit(solution)/shard_map/ppermute | solution.py:24
  47.5 4.4 %collective-permute-start.9 = (bf16[1,48,512]{2,1,0:T(8,128)(2,1)S(1)}, bf16[1,48,512]{2,1,0:T(8,128)(2,1)S(1)}, u32[]{:S(2)}, u32[]{:S(2)}) collective-permute-start(bf16[1,48,512]{2,1,0:T(8,128)(2,1)S(1)} %collective-permute-done.7), channel_id=1, source_target_pairs={{0,4},{4,8},{8,12},{12,16},{16,20},{20,24},{24,28},{28,0},{1,5},{5... | collective-permute-start | bytes 147464 | tf_op jit(solution)/shard_map/ppermute | solution.py:19
  47.5 4.4 %collective-permute-start.10 = (bf16[1,48,512]{2,1,0:T(8,128)(2,1)S(1)}, bf16[1,48,512]{2,1,0:T(8,128)(2,1)S(1)}, u32[]{:S(2)}, u32[]{:S(2)}) collective-permute-start(bf16[1,48,512]{2,1,0:T(8,128)(2,1)S(1)} %collective-permute-done.8), channel_id=1, source_target_pairs={{0,28},{4,0},{8,4},{12,8},{16,12},{20,16},{24,20},{28,24},{1,29},{... | collective-permute-start | bytes 147464 | tf_op jit(solution)/shard_map/ppermute | solution.py:24
  51.9 4.4 %collective-permute-start.11 = (bf16[1,48,512]{2,1,0:T(8,128)(2,1)S(1)}, bf16[1,48,512]{2,1,0:T(8,128)(2,1)S(1)}, u32[]{:S(2)}, u32[]{:S(2)}) collective-permute-start(bf16[1,48,512]{2,1,0:T(8,128)(2,1)S(1)} %collective-permute-done.9), channel_id=1, source_target_pairs={{0,4},{4,8},{8,12},{12,16},{16,20},{20,24},{24,28},{28,0},{1,5},{5... | collective-permute-start | bytes 147464 | tf_op jit(solution)/shard_map/ppermute | solution.py:19
  52.0 5.0 %collective-permute-start.12 = (bf16[1,48,512]{2,1,0:T(8,128)(2,1)S(1)}, bf16[1,48,512]{2,1,0:T(8,128)(2,1)S(1)}, u32[]{:S(2)}, u32[]{:S(2)}) collective-permute-start(bf16[1,48,512]{2,1,0:T(8,128)(2,1)S(1)} %collective-permute-done.10), channel_id=1, source_target_pairs={{0,28},{4,0},{8,4},{12,8},{16,12},{20,16},{24,20},{28,24},{1,29},{... | collective-permute-start | bytes 147464 | tf_op jit(solution)/shard_map/ppermute | solution.py:24
  56.3 4.4 %collective-permute-start.13 = (bf16[1,48,512]{2,1,0:T(8,128)(2,1)S(1)}, bf16[1,48,512]{2,1,0:T(8,128)(2,1)S(1)}, u32[]{:S(2)}, u32[]{:S(2)}) collective-permute-start(bf16[1,48,512]{2,1,0:T(8,128)(2,1)S(1)} %collective-permute-done.11), channel_id=1, source_target_pairs={{0,4},{4,8},{8,12},{12,16},{16,20},{20,24},{24,28},{28,0},{1,5},{5... | collective-permute-start | bytes 147464 | tf_op jit(solution)/shard_map/ppermute | solution.py:19
  70.9 6.8 %collective-permute-start.14 = (f32[48,512]{1,0:T(8,128)S(1)}, f32[48,512]{1,0:T(8,128)S(1)}, u32[]{:S(2)}, u32[]{:S(2)}) collective-permute-start(f32[48,512]{1,0:T(8,128)S(1)} %add.525), channel_id=1, source_target_pairs={{0,4},{4,8},{8,12},{12,16},{16,20},{20,24},{24,28},{1,5},{5,9},{9,... | collective-permute-start | bytes 294920 | tf_op jit(solution)/shard_map/ppermute | solution.py:50
  77.9 5.6 %collective-permute-start.15 = (f32[8,512]{1,0:T(8,128)S(1)}, f32[8,512]{1,0:T(8,128)S(1)}, u32[]{:S(2)}, u32[]{:S(2)}) collective-permute-start(f32[8,512]{1,0:T(8,128)S(1)} %get-tuple-element.97), channel_id=1, source_target_pairs={{0,1},{1,2},{2,3},{3,0},{4,5},{5,6},{6,7},{7,4},{8,9},{9,10},{10,1... | collective-permute-start | bytes 49160 | tf_op jit(solution)/shard_map/ppermute | solution.py:38
  90.0 6.8 %collective-permute-start.17 = (f32[48,512]{1,0:T(8,128)S(1)}, f32[48,512]{1,0:T(8,128)S(1)}, u32[]{:S(2)}, u32[]{:S(2)}) collective-permute-start(f32[48,512]{1,0:T(8,128)S(1)} %fusion.185), channel_id=1, source_target_pairs={{0,4},{4,8},{8,12},{12,16},{16,20},{20,24},{24,28},{1,5},{5,9},{9,... | collective-permute-start | bytes 294920 | tf_op jit(solution)/shard_map/ppermute | solution.py:50
  96.9 5.8 %collective-permute-start.18 = (f32[8,512]{1,0:T(8,128)S(1)}, f32[8,512]{1,0:T(8,128)S(1)}, u32[]{:S(2)}, u32[]{:S(2)}) collective-permute-start(f32[8,512]{1,0:T(8,128)S(1)} %get-tuple-element.95), channel_id=1, source_target_pairs={{0,1},{1,2},{2,3},{3,0},{4,5},{5,6},{6,7},{7,4},{8,9},{9,10},{10,1... | collective-permute-start | bytes 49160 | tf_op jit(solution)/shard_map/ppermute | solution.py:38
  110.0 4.4 %collective-permute-start.20 = (bf16[1,48,512]{2,1,0:T(8,128)(2,1)S(1)}, bf16[1,48,512]{2,1,0:T(8,128)(2,1)S(1)}, u32[]{:S(2)}, u32[]{:S(2)}) collective-permute-start(bf16[1,48,512]{2,1,0:T(8,128)(2,1)S(1)} %get-tuple-element.108), channel_id=1, source_target_pairs={{0,4},{4,8},{8,12},{12,16},{16,20},{20,24},{24,28},{28,0},{1,5},{5... | collective-permute-start | bytes 147464 | tf_op jit(solution)/shard_map/ppermute | solution.py:19
  110.0 5.0 %collective-permute-start.21 = (bf16[1,48,512]{2,1,0:T(8,128)(2,1)S(1)}, bf16[1,48,512]{2,1,0:T(8,128)(2,1)S(1)}, u32[]{:S(2)}, u32[]{:S(2)}) collective-permute-start(bf16[1,48,512]{2,1,0:T(8,128)(2,1)S(1)} %get-tuple-element.108), channel_id=1, source_target_pairs={{0,28},{4,0},{8,4},{12,8},{16,12},{20,16},{24,20},{28,24},{1,29},{... | collective-permute-start | bytes 147464 | tf_op jit(solution)/shard_map/ppermute | solution.py:24
  114.4 4.4 %collective-permute-start.22 = (bf16[1,48,512]{2,1,0:T(8,128)(2,1)S(1)}, bf16[1,48,512]{2,1,0:T(8,128)(2,1)S(1)}, u32[]{:S(2)}, u32[]{:S(2)}) collective-permute-start(bf16[1,48,512]{2,1,0:T(8,128)(2,1)S(1)} %collective-permute-done.20), channel_id=1, source_target_pairs={{0,4},{4,8},{8,12},{12,16},{16,20},{20,24},{24,28},{28,0},{1,5},{5... | collective-permute-start | bytes 147464 | tf_op jit(solution)/shard_map/ppermute | solution.py:19
  118.8 4.4 %collective-permute-start.24 = (bf16[1,48,512]{2,1,0:T(8,128)(2,1)S(1)}, bf16[1,48,512]{2,1,0:T(8,128)(2,1)S(1)}, u32[]{:S(2)}, u32[]{:S(2)}) collective-permute-start(bf16[1,48,512]{2,1,0:T(8,128)(2,1)S(1)} %collective-permute-done.22), channel_id=1, source_target_pairs={{0,4},{4,8},{8,12},{12,16},{16,20},{20,24},{24,28},{28,0},{1,5},{5... | collective-permute-start | bytes 147464 | tf_op jit(solution)/shard_map/ppermute | solution.py:19
  123.2 4.4 %collective-permute-start.26 = (bf16[1,48,512]{2,1,0:T(8,128)(2,1)S(1)}, bf16[1,48,512]{2,1,0:T(8,128)(2,1)S(1)}, u32[]{:S(2)}, u32[]{:S(2)}) collective-permute-start(bf16[1,48,512]{2,1,0:T(8,128)(2,1)S(1)} %collective-permute-done.24), channel_id=1, source_target_pairs={{0,4},{4,8},{8,12},{12,16},{16,20},{20,24},{24,28},{28,0},{1,5},{5... | collective-permute-start | bytes 147464 | tf_op jit(solution)/shard_map/ppermute | solution.py:19
  136.9 6.8 %collective-permute-start.27 = (f32[48,512]{1,0:T(8,128)S(1)}, f32[48,512]{1,0:T(8,128)S(1)}, u32[]{:S(2)}, u32[]{:S(2)}) collective-permute-start(f32[48,512]{1,0:T(8,128)S(1)} %add.574), channel_id=1, source_target_pairs={{0,4},{4,8},{8,12},{12,16},{16,20},{20,24},{24,28},{1,5},{5,9},{9,... | collective-permute-start | bytes 294920 | tf_op jit(solution)/shard_map/ppermute | solution.py:50
  143.9 5.6 %collective-permute-start.28 = (f32[8,512]{1,0:T(8,128)S(1)}, f32[8,512]{1,0:T(8,128)S(1)}, u32[]{:S(2)}, u32[]{:S(2)}) collective-permute-start(f32[8,512]{1,0:T(8,128)S(1)} %get-tuple-element.93), channel_id=1, source_target_pairs={{0,1},{1,2},{2,3},{3,0},{4,5},{5,6},{6,7},{7,4},{8,9},{9,10},{10,1... | collective-permute-start | bytes 49160 | tf_op jit(solution)/shard_map/ppermute | solution.py:38
  (20 other events, 126.2 us)
